TPU v7x, 32 devices: a whole 2x2x4 slice. The times are simulated.
32 devices in a mesh: enc: 4 (over x, core), own: 8 (over z, y).
Axes of the slice: x: 2, y: 2, z: 4, core: 2. Of those that a mesh axis runs over, the one named last changes fastest.
Arguments:
- features: bfloat16 [2048, 768], P(('enc', 'own')), may hold values from -6 to 6
- doc_cluster: int32 [2048], P(('enc', 'own')), may hold values from 0 to 31, as said below
- norm_gain: float32 [768], replicated, may hold values from 0.25 to 1.75
- w_in: bfloat16 [768, 3072], replicated, may hold values from -0.21875 to 0.21875
- b_in: float32 [3072], replicated, may hold values from -3 to 3
- w_out: bfloat16 [3072, 768], replicated, may hold values from -0.109375 to 0.109375
- members: bfloat16 [8, 4096, 768], P('own', 'enc'), may hold values from -6 to 6
- member_cluster: int32 [8, 4096], P('own', 'enc'), may hold values from 0 to 31, as said below
- cluster_range: int32 [32, 2], replicated, may hold values from 0 to 7, as said below
Outputs:
- embeddings: bfloat16 [2048, 768], P(('enc', 'own'))
- maxsim: float32 [2048], P(('enc', 'own'))
Inputs may be any that keep to these rules, and one draw needn't show every extreme that they name: `doc_cluster`: document k of a device's 64 belongs to a cluster whose range lies in owner group g = k mod (2), the owners 4 g to 4 g + 3. Of one device's documents at most 32 belong to clusters whose range holds a given owner; on every device some owner gets exactly 32. `cluster_range`: each cluster's range is an aligned run of 1, 2 or 4 owners inside an aligned group of four owners; every such group has a cluster that spans all four. `member_cluster`: A member's cluster has a range that holds the member's owner, and every owner in a cluster's range holds members of it.
All inputs are finite; a program needn't handle non-finite values.
Results may differ from a plain program's by a relative error of at most 0.0047.
Values may be sent and summed in bfloat16 or wider, within the bound.
No kernel may reach another device: no remote copies, remote signals or barrier semaphores. Data moves between devices by JAX's collectives and lax.ppermute only.
A program may use at most 64 MiB of HBM per device.

v0:
```python
import math

import jax
import jax.numpy as jnp
from jax import lax
from jax.sharding import PartitionSpec as P

lowest_score = -1e30


def best_match(rows, labels, stored, stored_labels):
    count = rows.shape[0]
    total = stored.shape[0]
    width = rows.shape[1]
    row_block = 2048 if count % 2048 == 0 else count
    col_block = 1024
    scale = 1.0 / math.sqrt(width)
    stored_blocks = stored.reshape(total // col_block, col_block, width)
    label_blocks = stored_labels.reshape(total // col_block, col_block)

    def one_block(group):
        block, block_labels = group

        def advance(best, pieces):
            stock, stock_labels = pieces
            score = (
                lax.dot_general(
                    block, stock, (((1,), (1,)), ((), ())), preferred_element_type=jnp.float32
                )
                * scale
            )
            score = jnp.where(block_labels[:, None] == stock_labels[None, :], score, lowest_score)
            return (jnp.maximum(best, jnp.max(score, axis=1)), None)

        start = jnp.full((block.shape[0],), lowest_score, jnp.float32)
        best, unused = lax.scan(advance, start, (stored_blocks, label_blocks))
        return best

    result = lax.map(
        one_block,
        (
            rows.reshape(count // row_block, row_block, width),
            labels.reshape(count // row_block, row_block),
        ),
    )
    return result.reshape(count)


def shards(
    features, doc_cluster, norm_gain, w_in, b_in, w_out, members, member_cluster, cluster_range
):
    inputs = features.astype(jnp.float32)
    center = inputs - jnp.mean(inputs, axis=1, keepdims=True)
    spread = jnp.mean(center * center, axis=1, keepdims=True)
    normed = (center * lax.rsqrt(spread + 1e-05) * norm_gain).astype(jnp.bfloat16)
    hidden = jax.nn.gelu(
        jnp.dot(normed, w_in, preferred_element_type=jnp.float32) + b_in, approximate=True
    ).astype(jnp.bfloat16)
    output = inputs + jnp.dot(hidden, w_out, preferred_element_type=jnp.float32)
    embeddings = (
        output * lax.rsqrt(jnp.mean(output * output, axis=1, keepdims=True) + 1e-06)
    ).astype(jnp.bfloat16)
    owners_count = lax.axis_size("own")
    encoders = lax.axis_size("enc")
    docs_here = features.shape[0]
    width = features.shape[1]
    capacity = docs_here * 4 // owners_count
    clusters = cluster_range.shape[0]
    onehot = (doc_cluster[:, None] == jnp.arange(clusters, dtype=jnp.int32)[None, :]).astype(
        jnp.int32
    )
    lowest = jnp.sum(onehot * cluster_range[None, :, 0], axis=1)
    highest = jnp.sum(onehot * cluster_range[None, :, 1], axis=1)
    owner_index = jnp.arange(owners_count, dtype=jnp.int32)
    covers = (owner_index[None, :] >= lowest[:, None]) & (owner_index[None, :] <= highest[:, None])
    flags = covers.astype(jnp.int32)
    position = jnp.cumsum(flags, axis=0) - flags
    slots = owner_index[None, :] * capacity + position
    target = jnp.where(covers, slots, owners_count * capacity)
    sources = jnp.broadcast_to(jnp.arange(docs_here, dtype=jnp.int32)[:, None], covers.shape)
    root = (
        jnp.full((owners_count * capacity + 1,), -1, jnp.int32)
        .at[target.reshape(-1)]
        .set(sources.reshape(-1))[:-1]
    )
    filled = root >= 0
    safe = jnp.maximum(root, 0)
    send_rows = jnp.where(filled[:, None], embeddings[safe], jnp.zeros((), jnp.bfloat16)).reshape(
        owners_count, capacity, width
    )
    send_labels = jnp.where(filled, doc_cluster[safe], -1).reshape(owners_count, capacity)
    copies = jnp.broadcast_to(send_rows[None], (encoders, owners_count, capacity, width)).reshape(
        encoders * owners_count, capacity, width
    )
    copy_labels = jnp.broadcast_to(send_labels[None], (encoders, owners_count, capacity)).reshape(
        encoders * owners_count, capacity
    )
    stored = members.reshape(-1, width)
    stored_labels = member_cluster.reshape(-1)
    rows = lax.all_to_all(copies, ("enc", "own"), split_axis=0, concat_axis=0, tiled=True)
    labels = lax.all_to_all(copy_labels, ("enc", "own"), split_axis=0, concat_axis=0, tiled=True)
    senders = labels.shape[0]
    items = labels.shape[1]
    best = best_match(
        rows.reshape(senders * items, width), labels.reshape(-1), stored, stored_labels
    ).reshape(senders, items)
    replies = lax.all_to_all(best, ("enc", "own"), split_axis=0, concat_axis=0, tiled=True)
    returned = jnp.max(replies.reshape(encoders, owners_count, capacity), axis=0)
    picked = returned.reshape(-1)[jnp.where(covers, slots, 0)]
    maxsim = jnp.max(jnp.where(covers, picked, lowest_score), axis=1)
    return (embeddings, maxsim)


def solution(mesh):
    placed = (
        P(("enc", "own"), None),
        P(("enc", "own")),
        P(),
        P(),
        P(),
        P(),
        P("own", "enc", None),
        P("own", "enc"),
        P(),
    )
    return jax.shard_map(
        shards,
        mesh=mesh,
        in_specs=placed,
        out_specs=(P(("enc", "own"), None), P(("enc", "own"))),
        check_vma=False,
    )
```

profile of v0, /device:TPU:0, one launch (start us, length us, event | category | flops | bytes accessed | tf_op | source)
XLA Modules:
  0.0 87.4 jit_solution(17483637820065243426)
XLA Ops:
  0.6 0.0 copy-start
  0.7 0.8 slice_bitcast_fusion
  1.5 0.1 add.113
  1.6 0.1 reshape.319
  1.7 0.7 select_reduce_fusion.3
  2.4 0.1 fusion.37
  2.5 0.1 reduce_window_sum.15
  2.6 0.1 reduce_window_sum.16
  2.7 0.1 and.24
  2.8 2.4 %scatter_custom_fusion = s32[257]{0:T(512)S(1)} fusion(s32[512]{0:T(512)S(1)} %bitcast.33, s32[512]{0:T(512)S(1)} %reshape.319, s32[]{:T(128)} %constant.72.clone.1), kind=kCustom, calls=%fused_computation.55 | custom fusion | bytes 1032 | tf_op jit(solution)/shard_map/scatter | solution.py:84
  5.3 0.1 ge.55
  5.4 1.9 %gather_fusion = s32[256]{0:T(256)S(1)} fusion(s32[64]{0:T(128)} %param.10, s32[1024]{0:T(1024)S(1)} %pad_clamp_fusion.1), kind=kCustom, calls=%fused_computation | custom fusion | bytes 3072 | tf_op jit(solution)/shard_map/gather | solution.py:91
  7.3 0.1 gather.14
  7.4 0.6 broadcast_in_dim.86
  8.0 7.3 %all-to-all-start = ((s32[32,1,32]{2,1,0:T(1,128)}), s32[32,1,32]{2,1,0:T(1,128)S(1)}, u32[]{:S(2)}, u32[]{:S(2)}) async-start(s32[32,1,32]{2,1,0:T(1,128)} %bitcast.3), calls=%async_computation | async-start | bytes 32768 | tf_op jit(solution)/shard_map/all_to_all | solution.py:101
  15.3 1.0 %convert_reduce_fusion = f32[64]{0:T(128)S(1)} fusion(bf16[64,768]{1,0:T(8,128)(2,1)} %param.9), kind=kLoop, calls=%fused_computation.24 | loop fusion | flops 98240 | bytes 98560 | tf_op jit(solution)/shard_map/reduce_sum | solution.py:53
  16.3 1.1 %fusion.16 = f32[64]{0:T(128)S(1)} fusion(bf16[64,768]{1,0:T(8,128)(2,1)} %param.9, f32[64]{0:T(128)S(1)} %broadcast_multiply_fusion), kind=kLoop, calls=%fused_computation.27 | loop fusion | flops 196544 | bytes 98816 | tf_op jit(solution)/shard_map/reduce_sum | solution.py:54
  17.4 5.9 %multiply_reduce_fusion = (f32[64]{0:T(128)S(1)}, f32[64,768]{1,0:T(8,128)S(1)}) fusion(bf16[3072,768]{1,0:T(8,128)(2,1)} %param.14, bf16[768,3072]{1,0:T(8,128)(2,1)} %param.12, f32[3072]{0:T(1024)} %param.13, bf16[64,768]{1,0:T(8,128)(2,1)} %param.9, f32[768]{0:T(1024)} %param.11, f32[64]{0:T(128)S(1)} %add_rsqrt_fusion.1, f32[64]{0:T(128)S(1)} %broadcast_multiply_fusion), kind=kOutput, calls=%fused_computation.31 | convolution fusion | flops 606388160 | bytes 9748224 | tf_op jit(solution)/shard_map/dot_general | solution.py:59
  23.4 0.1 multiply_convert_fusion
  23.5 0.0 copy-start.1
  23.5 0.0 copy-start.2
  23.5 1.2 %gather_fusion.1 = bf16[256,768]{1,0:T(8,128)(2,1)S(1)} fusion(bf16[64,768]{1,0:T(8,128)(2,1)S(1)} %multiply_convert_fusion, s32[1024]{0:T(1024)S(1)} %pad_clamp_fusion.1), kind=kCustom, calls=%fused_computation.1 | custom fusion | bytes 787456 | tf_op jit(solution)/shard_map/gather | solution.py:88
  24.7 0.1 broadcast_select_fusion
  24.8 0.0 all-to-all-done
  24.8 1.3 %broadcast_in_dim.89 = bf16[4,8,32,768]{3,2,1,0:T(8,128)(2,1)} broadcast(bf16[8,32,768]{2,1,0:T(8,128)(2,1)S(1)} %broadcast_select_fusion), dimensions={1,2,3} | broadcast | bytes 1966080 | tf_op jit(solution)/shard_map/broadcast_in_dim | solution.py:92
  26.1 0.0 copy-done.1
  26.1 5.8 %all-to-all-start.1 = ((bf16[32,32,768]{2,1,0:T(8,128)(2,1)}), bf16[32,32,768]{2,1,0:T(8,128)(2,1)S(1)}, u32[]{:S(2)}, u32[]{:S(2)}) async-start(bf16[32,32,768]{2,1,0:T(8,128)(2,1)} %bitcast.6), calls=%async_computation.1 | async-start | bytes 3145728 | tf_op jit(solution)/shard_map/all_to_all | solution.py:100
  32.0 0.1 compare_select_fusion
  32.1 0.1 reshape.309
  32.2 0.5 broadcast.235
  32.7 0.7 reduce.3
  33.4 0.1 eq.47
  33.4 37.3 %all-to-all-done.1 = bf16[32,32,768]{2,1,0:T(8,128)(2,1)S(1)} async-done(((bf16[32,32,768]{2,1,0:T(8,128)(2,1)}), bf16[32,32,768]{2,1,0:T(8,128)(2,1)S(1)}, u32[]{:S(2)}, u32[]{:S(2)}) %all-to-all-start.1) | async-done | bytes 1572896 | tf_op jit(solution)/shard_map/all_to_all | solution.py:100
  70.8 0.0 copy-done
  70.8 0.0 copy-done.2
  70.8 1.8 %select_reduce_fusion = f32[1024]{0:T(1024)S(1)} fusion(bf16[1024,768]{1,0:T(8,128)(2,1)S(1)} %bitcast.30, s32[1024]{0:T(1024)S(1)} %eq.47, s32[1024]{0:T(1024)S(1)} %bitcast.34, bf16[1,1024,768]{2,1,0:T(8,128)(2,1)S(1)} %copy-done), kind=kOutput, calls=%fused_computation.4 | convolution fusion | flops 1614806016 | bytes 3158016 | tf_op jit(solution)/shard_map/while/body/eval_jaxpr/while/body/eval_jaxpr/dot_general | solution.py:27
  72.6 0.7 max.21
  73.3 2.6 %all-to-all-start.2 = ((f32[32,1,32]{2,1,0:T(1,128)}), f32[32,1,32]{2,1,0:T(1,128)S(1)}, u32[]{:S(2)}, u32[]{:S(2)}) async-start(f32[32,1,32]{2,1,0:T(1,128)} %max.21), calls=%async_computation.2 | async-start | bytes 32768 | tf_op jit(solution)/shard_map/all_to_all | solution.py:107
  75.9 7.1 %all-to-all-done.2 = f32[32,1,32]{2,1,0:T(1,128)S(1)} async-done(((f32[32,1,32]{2,1,0:T(1,128)}), f32[32,1,32]{2,1,0:T(1,128)S(1)}, u32[]{:S(2)}, u32[]{:S(2)}) %all-to-all-start.2) | async-done | bytes 4128 | tf_op jit(solution)/shard_map/all_to_all | solution.py:107
  83.0 0.1 reshape.290
  83.1 3.5 %gather_fusion.2 = f32[512]{0:T(512)S(1)} fusion(f32[256]{0:T(256)S(1)} %reshape.290, s32[1024]{0:T(1024)S(1)} %pad_clamp_fusion), kind=kCustom, calls=%fused_computation.2 | custom fusion | bytes 6144 | tf_op jit(solution)/shard_map/gather | solution.py:109
  86.6 0.1 reshape.308
  86.7 0.7 select_reduce_fusion.1
  (14 shorter events, 0.1 us)
Async XLA Ops:
  0.6 70.2 %copy-start = (bf16[1,1024,768]{2,1,0:T(8,128)(2,1)S(1)}, bf16[1,1024,768]{2,1,0:T(8,128)(2,1)}, u32[]{:S(2)}) copy-start(bf16[1,1024,768]{2,1,0:T(8,128)(2,1)} %param.15) | copy-start | bytes 4718596
  8.0 16.8 %all-to-all-start = ((s32[32,1,32]{2,1,0:T(1,128)}), s32[32,1,32]{2,1,0:T(1,128)S(1)}, u32[]{:S(2)}, u32[]{:S(2)}) async-start(s32[32,1,32]{2,1,0:T(1,128)} %bitcast.3), calls=%async_computation | async-start | bytes 32768 | tf_op jit(solution)/shard_map/all_to_all | solution.py:101
  23.5 2.7 %copy-start.1 = (bf16[64,768]{1,0:T(8,128)(2,1)}, bf16[64,768]{1,0:T(8,128)(2,1)S(1)}, u32[]{:S(2)}) copy-start(bf16[64,768]{1,0:T(8,128)(2,1)S(1)} %multiply_convert_fusion) | copy-start | bytes 294916
  23.5 47.3 %copy-start.2 = (s32[1,1024]{1,0:T(1,128)S(1)}, s32[1,1024]{1,0:T(1,128)}, u32[]{:S(2)}) copy-start(s32[1,1024]{1,0:T(1,128)} %param.16) | copy-start | bytes 12292
  26.1 44.6 %all-to-all-start.1 = ((bf16[32,32,768]{2,1,0:T(8,128)(2,1)}), bf16[32,32,768]{2,1,0:T(8,128)(2,1)S(1)}, u32[]{:S(2)}, u32[]{:S(2)}) async-start(bf16[32,32,768]{2,1,0:T(8,128)(2,1)} %bitcast.6), calls=%async_computation.1 | async-start | bytes 3145728 | tf_op jit(solution)/shard_map/all_to_all | solution.py:100
  73.3 9.7 %all-to-all-start.2 = ((f32[32,1,32]{2,1,0:T(1,128)}), f32[32,1,32]{2,1,0:T(1,128)S(1)}, u32[]{:S(2)}, u32[]{:S(2)}) async-start(f32[32,1,32]{2,1,0:T(1,128)} %max.21), calls=%async_computation.2 | async-start | bytes 32768 | tf_op jit(solution)/shard_map/all_to_all | solution.py:107
where the time goes:
time: 87.8 us; the launch traced here: 87.4 us
  waiting for transfers between devices  44.5 us (51%)
  starting transfers between devices  15.7 us (18%)
  local copies, waits for them, and re-layouts  13.9 us (16%)
  matrix products  7.76 us (9%)
  other arithmetic  4.76 us (5%)
    all_to_all x1, waiting for transfers between devices, shards(): lax.all_to_all(copies, ('enc', 'own'), split_axis=0, concat_axis=0, tiled...  37.3 us
    all_to_all x1, starting transfers between devices, shards(): lax.all_to_all(copy_labels, ('enc', 'own'), split_axis=0, concat_axis=0,...  7.33 us
    all_to_all x1, waiting for transfers between devices, shards(): lax.all_to_all(best, ('enc', 'own'), split_axis=0, concat_axis=0, tiled=T...  7.13 us
    dot_general x1, matrix products, shards(): output = inputs + jnp.dot(hidden, w_out, preferred_element_type=jnp.float32)  5.92 us
    all_to_all x1, starting transfers between devices, shards(): lax.all_to_all(copies, ('enc', 'own'), split_axis=0, concat_axis=0, tiled...  5.83 us
    gather x2, local copies, waits for them, and re-layouts, shards(): picked = returned.reshape(-1)[jnp.where(covers, slots, 0)]  3.58 us
    all_to_all x1, starting transfers between devices, shards(): lax.all_to_all(best, ('enc', 'own'), split_axis=0, concat_axis=0, tiled=T...  2.57 us
    scatter x1, local copies, waits for them, and re-layouts, shards(): root = jnp.full((owners_count * capacity + 1,), -1, jnp.int32).at[target....  2.44 us
  transfers between devices with their start and end apart: 3, of which 2 were waited for; matrix products, arithmetic and copies ran while one was open for 12% of the time, Pallas kernels for 0%

commit v1 on v0

v1 whole, which is shorter than its diff:
```python
import functools
import math

import jax
import jax.numpy as jnp
from jax import lax
from jax.experimental import pallas as pl
from jax.experimental.pallas import tpu as pltpu
from jax.sharding import PartitionSpec as P

lowest_score = -1e30
quad = 4
lanes = 128
pad_rows = 16


def whole_spec(space=pltpu.VMEM):
    return pl.BlockSpec(memory_space=space)


def encode_kernel(
    groups,
    features,
    labels,
    gain,
    w_in,
    b_in,
    w_out,
    embeddings,
    own_out,
    cross_out,
    normed,
    total,
    columns,
):
    step = pl.program_id(0)
    docs, width = features.shape
    per = docs // groups

    @pl.when(step == 0)
    def _():
        inputs = features[...].astype(jnp.float32)
        center = inputs - jnp.mean(inputs, axis=1, keepdims=True)
        spread = jnp.mean(center * center, axis=1, keepdims=True)
        normed[...] = (center * lax.rsqrt(spread + 1e-05) * gain[...]).astype(jnp.bfloat16)
        total[...] = inputs

    hidden = jax.nn.gelu(
        jnp.dot(normed[...], w_in[...], preferred_element_type=jnp.float32) + b_in[...],
        approximate=True,
    ).astype(jnp.bfloat16)
    total[...] += jnp.dot(hidden, w_out[...], preferred_element_type=jnp.float32)

    @pl.when(step == pl.num_programs(0) - 1)
    def _():
        output = total[...]
        scaled = output * lax.rsqrt(jnp.mean(output * output, axis=1, keepdims=True) + 1e-06)
        embeddings[...] = scaled.astype(jnp.bfloat16)
        group = lax.axis_index("own") // quad
        blocks = width // lanes
        for block in range(blocks):
            columns[block] = scaled[:, block * lanes : (block + 1) * lanes]
        source = lax.broadcasted_iota(jnp.int32, (docs, lanes), 0)
        column = lax.broadcasted_iota(jnp.int32, (docs, lanes), 1)
        label_rows = jnp.broadcast_to(labels[...].astype(jnp.float32), (pad_rows, docs)).astype(
            jnp.bfloat16
        )
        for shift in range(groups):
            residue = lax.rem(group + shift, groups)
            pick = (source == (column % per) * groups + residue).astype(jnp.bfloat16)
            tags = jnp.dot(label_rows, pick, preferred_element_type=jnp.float32).astype(
                jnp.bfloat16
            )
            for block in range(blocks):
                piece = jnp.zeros((per, lanes), jnp.float32)
                for choice in range(groups):
                    piece = jnp.where(
                        residue == choice,
                        columns[block, pl.ds(choice, per, stride=groups), :],
                        piece,
                    )
                piece = piece.astype(jnp.bfloat16)
                if shift == 0:
                    for peer in range(own_out.shape[0]):
                        own_out[peer, 0, pl.ds(block * per, per), :] = piece
                else:
                    cross_out[shift - 1, pl.ds(block * per, per), :] = piece
            if shift == 0:
                for peer in range(own_out.shape[0]):
                    own_out[peer, 0, pl.ds(blocks * per, pad_rows), :] = tags
            else:
                cross_out[shift - 1, pl.ds(blocks * per, pad_rows), :] = tags


def encode(features, doc_cluster, norm_gain, w_in, b_in, w_out, groups, peers):
    docs, width = features.shape
    hidden = w_in.shape[1]
    chunk = 512 if hidden % 512 == 0 else hidden
    per = docs // groups
    rows = width // lanes * per + pad_rows
    return pl.pallas_call(
        functools.partial(encode_kernel, groups),
        grid=(hidden // chunk,),
        in_specs=[
            pl.BlockSpec((docs, width), lambda i: (0, 0)),
            pl.BlockSpec((1, docs), lambda i: (0, 0)),
            pl.BlockSpec((1, width), lambda i: (0, 0)),
            pl.BlockSpec((width, chunk), lambda i: (0, i)),
            pl.BlockSpec((1, chunk), lambda i: (0, i)),
            pl.BlockSpec((chunk, width), lambda i: (i, 0)),
        ],
        out_specs=[
            pl.BlockSpec((docs, width), lambda i: (0, 0)),
            pl.BlockSpec((peers, 1, rows, lanes), lambda i: (0, 0, 0, 0)),
            pl.BlockSpec((groups - 1, rows, lanes), lambda i: (0, 0, 0)),
        ],
        out_shape=[
            jax.ShapeDtypeStruct((docs, width), jnp.bfloat16),
            jax.ShapeDtypeStruct((peers, 1, rows, lanes), jnp.bfloat16),
            jax.ShapeDtypeStruct((groups - 1, rows, lanes), jnp.bfloat16),
        ],
        scratch_shapes=[
            pltpu.VMEM((docs, width), jnp.bfloat16),
            pltpu.VMEM((docs, width), jnp.float32),
            pltpu.VMEM((width // lanes, docs, lanes), jnp.float32),
        ],
        cost_estimate=pl.CostEstimate(
            flops=4 * docs * width * hidden,
            bytes_accessed=4 * width * hidden,
            transcendentals=docs * hidden,
        ),
        compiler_params=pltpu.CompilerParams(vmem_limit_bytes=24 << 20),
        name="encode",
    )(
        features,
        doc_cluster.reshape(1, docs),
        norm_gain.reshape(1, width),
        pltpu.with_memory_space_constraint(w_in, pltpu.HBM),
        b_in.reshape(1, hidden),
        pltpu.with_memory_space_constraint(w_out, pltpu.HBM),
    )


def tags_kernel(ranges, mine, theirs, out):
    owner = lax.axis_index("own")
    clusters = ranges.shape[0]
    row = 0
    for labels in (mine, theirs):
        value = labels[...]
        inside = jnp.zeros(value.shape, jnp.bool_)
        for cluster in range(clusters):
            held = (ranges[cluster, 0] <= owner) & (owner <= ranges[cluster, 1])
            inside = inside | (value == jnp.where(held, cluster, -2))
        value = jnp.where(inside, value, -1).astype(jnp.float32)
        for line in range(value.shape[0]):
            tall = jnp.broadcast_to(value[line : line + 1, :], (lanes, lanes)).T
            out[pl.ds(row, lanes), :] = tall
            row += lanes


def member_tags(cluster_range, mine, theirs):
    total = mine.size
    return pl.pallas_call(
        tags_kernel,
        in_specs=[whole_spec(pltpu.SMEM), whole_spec(), whole_spec()],
        out_specs=whole_spec(),
        out_shape=jax.ShapeDtypeStruct((2 * total, lanes), jnp.float32),
        cost_estimate=pl.CostEstimate(
            flops=total * lanes, bytes_accessed=8 * total * lanes, transcendentals=0
        ),
        compiler_params=pltpu.CompilerParams(vmem_limit_bytes=4 << 20),
        name="tags",
    )(cluster_range, mine.reshape(-1, lanes), theirs.reshape(-1, lanes))


def best_rows(payload, tags, stores, width):
    peers, slots, rows, unused = payload.shape
    blocks = width // lanes
    per = (rows - pad_rows) // blocks
    count = peers * slots * per
    docs = jnp.concatenate(
        [
            payload[:, :, pl.ds(block * per, per), :].reshape(count, lanes)
            for block in range(blocks)
        ],
        axis=1,
    )
    column = lax.broadcasted_iota(jnp.int32, (1, lanes), 1) // per
    wanted = []
    for start in range(0, count, lanes):
        row = jnp.zeros((1, lanes), jnp.float32)
        for part in range(lanes // per):
            peer, slot = divmod(start // per + part, slots)
            row = jnp.where(
                column == part,
                payload[peer, slot, pl.ds(blocks * per, pad_rows), :][0:1].astype(jnp.float32),
                row,
            )
        wanted.append(row)
    best = [jnp.full((8, lanes), lowest_score, jnp.float32) for unused in wanted]
    tall = 256
    first = 0
    for store in stores:
        for start in range(0, store.shape[0], tall):
            score = lax.dot_general(
                store[pl.ds(start, tall), :],
                docs,
                (((1,), (1,)), ((), ())),
                preferred_element_type=jnp.float32,
            )
            held = tags[pl.ds(first, tall), :]
            first += tall
            for index, row in enumerate(wanted):
                piece = jnp.where(
                    held == row, score[:, index * lanes : (index + 1) * lanes], lowest_score
                )
                best[index] = jnp.maximum(
                    best[index], jnp.max(piece.reshape(tall // 8, 8, lanes), axis=0)
                )
    return [jnp.max(piece, axis=0, keepdims=True) for piece in best]


def own_kernel(payload, tags, mine, theirs, out):
    for index, row in enumerate(best_rows(payload, tags, (mine, theirs), mine.shape[1])):
        out[pl.ds(index, 1), :] = row


def cross_kernel(groups, owners, payload, tags, mine, theirs, own_best, out):
    slots = groups - 1
    peers = payload.shape[0]
    blocks = mine.shape[1] // lanes
    per = (payload.shape[2] - pad_rows) // blocks
    found = best_rows(payload, tags, (mine, theirs), mine.shape[1])
    core = lax.rem(lax.axis_index("enc"), 2)
    group = lax.axis_index("own") // quad
    out[...] = jnp.zeros(out.shape, out.dtype)
    for peer in range(peers):
        across, lane_owner = divmod(peer, quad)
        for shift in range(groups):
            home = lax.rem(group + groups - shift, groups)
            target = (2 * across + core) * owners + home * quad + lane_owner
            if shift == 0:
                row = own_best[pl.ds(peer * per // lanes, 1), :]
            else:
                row = found[(peer * slots + shift - 1) * per // lanes]
            out[target] = row


def finish_kernel(groups, owners, per, scale, received, out):
    slots = groups - 1
    docs = out.shape[1]
    peers = received.shape[0] // (2 * groups)
    encoder = lax.axis_index("enc")
    owner = lax.axis_index("own")
    core = lax.rem(encoder, 2)
    group = owner // quad
    place = (encoder // 2) * quad + lax.rem(owner, quad)
    column = lax.broadcasted_iota(jnp.int32, (8, lanes), 1)
    result = jnp.zeros((8, lanes), jnp.float32)
    for source in range(groups):
        best = jnp.full((1, lanes), lowest_score, jnp.float32)
        for peer in range(peers):
            across, lane_owner = divmod(peer, quad)
            best = jnp.maximum(
                best, received[(2 * across + core) * owners + source * quad + lane_owner]
            )
        shift = lax.rem(source + groups - group, groups)
        position = jnp.where(shift == 0, place, place * slots + shift - 1) * per
        offset = lax.rem(position, lanes)
        index = lax.rem(offset + column // groups, lanes)
        taken = jnp.take_along_axis(jnp.broadcast_to(best, (8, lanes)), index, axis=1)
        result = jnp.where(column % groups == source, taken, result)
    out[...] = (result * scale)[0:1, 0:docs]


def shards(
    features, doc_cluster, norm_gain, w_in, b_in, w_out, members, member_cluster, cluster_range
):
    owners = lax.axis_size("own")
    encoders = lax.axis_size("enc")
    docs, width = features.shape
    groups = owners // quad
    per = docs // groups
    peers = encoders // 2 * quad
    axes = ("enc", "own")
    swap = [(index, index ^ 1) for index in range(encoders)]
    mine = members.reshape(-1, width)
    theirs = lax.ppermute(mine, "enc", swap)
    their_labels = lax.ppermute(member_cluster, "enc", swap)
    embeddings, own_rows, cross_rows = encode(
        features, doc_cluster, norm_gain, w_in, b_in, w_out, groups, peers
    )
    arrived = [
        lax.ppermute(
            cross_rows[shift - 1],
            "own",
            [(index, (index + quad * shift) % owners) for index in range(owners)],
        )
        for shift in range(1, groups)
    ]
    circles = [
        [
            (2 * across + core) * owners + group * quad + lane_owner
            for across in range(encoders // 2)
            for lane_owner in range(quad)
        ]
        for core in range(2)
        for group in range(groups)
    ]
    spread = functools.partial(
        lax.all_to_all,
        axis_name=axes,
        split_axis=0,
        concat_axis=0,
        axis_index_groups=circles,
        tiled=True,
    )
    own_all = spread(own_rows)
    stacked = jnp.stack(arrived)
    cross_all = spread(jnp.broadcast_to(stacked[None], (peers,) + stacked.shape))
    tags = member_tags(cluster_range, member_cluster, their_labels)
    count = peers * per
    cost = pl.CostEstimate(
        flops=4 * count * mine.shape[0] * width,
        bytes_accessed=4 * mine.shape[0] * width,
        transcendentals=0,
    )
    params = pltpu.CompilerParams(vmem_limit_bytes=24 << 20)
    own_best = pl.pallas_call(
        own_kernel,
        in_specs=[whole_spec()] * 4,
        out_specs=whole_spec(),
        out_shape=jax.ShapeDtypeStruct((count // lanes, lanes), jnp.float32),
        cost_estimate=cost,
        compiler_params=params,
        name="own_match",
    )(own_all, tags, mine, theirs)
    replies = pl.pallas_call(
        functools.partial(cross_kernel, groups, owners),
        in_specs=[whole_spec()] * 5,
        out_specs=whole_spec(),
        out_shape=jax.ShapeDtypeStruct((encoders * owners, 1, lanes), jnp.float32),
        cost_estimate=cost,
        compiler_params=params,
        name="cross_match",
    )(cross_all, tags, mine, theirs, own_best)
    received = lax.all_to_all(replies, axes, split_axis=0, concat_axis=0, tiled=True)
    maxsim = pl.pallas_call(
        functools.partial(finish_kernel, groups, owners, per, 1.0 / math.sqrt(width)),
        in_specs=[whole_spec()],
        out_specs=whole_spec(),
        out_shape=jax.ShapeDtypeStruct((1, docs), jnp.float32),
        name="finish",
    )(received)
    return (embeddings, maxsim.reshape(docs))


def solution(mesh):
    placed = (
        P(("enc", "own"), None),
        P(("enc", "own")),
        P(),
        P(),
        P(),
        P(),
        P("own", "enc", None),
        P("own", "enc"),
        P(),
    )
    return jax.shard_map(
        shards,
        mesh=mesh,
        in_specs=placed,
        out_specs=(P(("enc", "own"), None), P(("enc", "own"))),
        check_vma=False,
    )
```

time: 87.8 us -> 54.5 us (0.62)
  waiting for transfers between devices: 44.5 us -> 12 us
  Pallas kernels: 0 us -> 15.1 us
  local copies, waits for them, and re-layouts: 13.9 us -> 3.85 us
  blocking collectives: 0 us -> 9.45 us
  matrix products: 7.76 us -> 0 us
  other arithmetic: 4.76 us -> 0 us
  starting transfers between devices: 15.7 us -> 12.8 us
    all_to_all x3 -> x2, waiting for transfers between devices: 44.5 us -> 7.04 us  [the longest x1 4 us: shards(): own_all = spread(own_rows)]
    pallas_call x0 -> x5, Pallas kernels: none -> 15.1 us  [the longest x1 7.71 us: encode(): pl.pallas_call(functools.partial(encode_kernel, groups), grid=(hidden //...]
    all_to_all x0 -> x1, blocking collectives: none -> 9.45 us  [shards(): lax.all_to_all(replies, axes, split_axis=0, concat_axis=0, tiled=True)]
    dot_general x2 -> x0, matrix products: 7.76 us -> none  [the longest x1 5.92 us: shards(): output = inputs + jnp.dot(hidden, w_out, preferred_element_type=jnp.float32)]
    gather x5 -> x0, local copies, waits for them, and re-layouts: 6.74 us -> none  [the longest x2 3.58 us: shards(): picked = returned.reshape(-1)[jnp.where(covers, slots, 0)]]
    all_to_all x3 -> x2, starting transfers between devices: 15.7 us -> 9.61 us  [the longest x1 5.74 us: shards(): own_all = spread(own_rows)]
    ppermute x0 -> x3, waiting for transfers between devices: none -> 4.98 us  [the longest x1 3.93 us: shards(): lax.ppermute(cross_rows[shift - 1], 'own', [(index, (index + quad * shift...]
    ppermute x0 -> x3, starting transfers between devices: none -> 3.22 us  [the longest x1 2.59 us: shards(): lax.ppermute(cross_rows[shift - 1], 'own', [(index, (index + quad * shift...]
  transfers between devices with their start and end apart: 3 -> 5, of which waited for: 2 -> 4; matrix products, arithmetic and copies ran while one was open for 12% -> 3% of each run, Pallas kernels for 0% -> 21%
where the time goes in v1:
time: 54.5 us; the launch traced here: 53.9 us
  Pallas kernels  15.1 us (28%)
  starting transfers between devices  12.8 us (23%)
  waiting for transfers between devices  12 us (22%)
  blocking collectives  9.45 us (17%)
  local copies, waits for them, and re-layouts  3.85 us (7%)
  between operations  0.7 us (1%)
    all_to_all x1, blocking collectives, shards(): lax.all_to_all(replies, axes, split_axis=0, concat_axis=0, tiled=True)  9.45 us
    pallas_call x1, Pallas kernels, encode(): pl.pallas_call(functools.partial(encode_kernel, groups), grid=(hidden //...  7.71 us
    all_to_all x1, starting transfers between devices, shards(): own_all = spread(own_rows)  5.74 us
    all_to_all x1, waiting for transfers between devices, shards(): own_all = spread(own_rows)  4 us
    ppermute x1, waiting for transfers between devices, shards(): lax.ppermute(cross_rows[shift - 1], 'own', [(index, (index + quad * shift...  3.93 us
    all_to_all x1, starting transfers between devices, shards(): spread(jnp.broadcast_to(stacked[None], (peers,) + stacked.shape))  3.87 us
    all_to_all x1, waiting for transfers between devices, shards(): spread(jnp.broadcast_to(stacked[None], (peers,) + stacked.shape))  3.04 us
    ppermute x1, starting transfers between devices, shards(): lax.ppermute(cross_rows[shift - 1], 'own', [(index, (index + quad * shift...  2.59 us
  transfers between devices with their start and end apart: 5, of which 4 were waited for; matrix products, arithmetic and copies ran while one was open for 3% of the time, Pallas kernels for 21%

profile of v1, /device:TPU:0, one launch (start us, length us, event | category | flops | bytes accessed | tf_op | source)
XLA Modules:
  0.0 53.9 jit_solution(8761864284637356460)
XLA Ops:
  0.6 0.6 %collective-permute-start.2 = (bf16[1024,768]{1,0:T(8,128)(2,1)}, bf16[1024,768]{1,0:T(8,128)(2,1)}, u32[]{:S(2)}, u32[]{:S(2)}) collective-permute-start(bf16[1024,768]{1,0:T(8,128)(2,1)} %bitcast.7), channel_id=1, source_target_pairs={{0,8},{8,0},{16,24},{24,16},{1,9},{9,1},{17,25},{25,17},{2,10},{10... | collective-permute-start | bytes 4718600 | tf_op jit(solution)/shard_map/ppermute | solution.py:288
  1.2 0.7 %reshape.29.gain = f32[1,768]{1,0:T(1,128)S(1)} reshape(f32[768]{0:T(1024)} %param.11) | data formatting | bytes 6144 | tf_op jit(solution)/shard_map/reshape | solution.py:137
  1.9 0.0 copy-start.1
  1.9 0.9 %copy-done.1 = bf16[64,768]{1,0:T(8,128)(2,1)S(1)} copy-done((bf16[64,768]{1,0:T(8,128)(2,1)S(1)}, bf16[64,768]{1,0:T(8,128)(2,1)}, u32[]{:S(2)}) %copy-start.1) | copy-done | bytes 98328
  2.8 0.0 copy-start.2
  2.8 0.7 %copy-done.2 = f32[3072]{0:T(1024)S(1)} copy-done((f32[3072]{0:T(1024)S(1)}, f32[3072]{0:T(1024)}, u32[]{:S(2)}) %copy-start.2) | copy-done | bytes 12312
  3.5 0.0 copy-start.4
  3.5 0.7 %copy-done.4 = s32[64]{0:T(128)S(1)} copy-done((s32[64]{0:T(128)S(1)}, s32[64]{0:T(128)}, u32[]{:S(2)}) %copy-start.4) | copy-done | bytes 280
  4.1 0.0 copy-start.3
  4.1 0.0 copy-start.5
  4.1 0.0 copy-start
  4.1 7.7 %encode.1 = (bf16[64,768]{1,0:T(8,128)(2,1)}, bf16[8,1,208,128]{3,2,1,0:T(8,128)(2,1)}, bf16[1,208,128]{2,1,0:T(8,128)(2,1)S(1)}) custom-call(bf16[64,768]{1,0:T(8,128)(2,1)S(1)} %copy-done.1, s32[1,64]{1,0:T(1,128)S(1)} %bitcast.13, f32[1,768]{1,0:T(1,128)S(1)} %reshape.29.gain, bf16[768,3072]{1,0:T(8,128)(2,1)} %w_in.1, f32[1,3072]{1,0:T(1,128)S(1)} %bitcast.10, ...), custom_call_target="tpu_custom_call" | custom-call | flops 603979776 | bytes 9437184 | tf_op jit(solution)/shard_map/encode/pallas_call | solution.py:101
  11.8 5.7 %all-to-all-start.1 = ((bf16[8,1,208,128]{3,2,1,0:T(8,128)(2,1)}), bf16[8,1,208,128]{3,2,1,0:T(8,128)(2,1)S(1)}, u32[]{:S(2)}, u32[]{:S(2)}) async-start(bf16[8,1,208,128]{3,2,1,0:T(8,128)(2,1)} %get-tuple-element.7), calls=%async_computation.1 | async-start | bytes 851968 | tf_op jit(solution)/shard_map/all_to_all | solution.py:318
  17.6 2.6 %collective-permute-start = (bf16[208,128]{1,0:T(8,128)(2,1)S(1)}, bf16[208,128]{1,0:T(8,128)(2,1)S(1)}, u32[]{:S(2)}, u32[]{:S(2)}) collective-permute-start(bf16[208,128]{1,0:T(8,128)(2,1)S(1)} %bitcast.14), channel_id=1, source_target_pairs={{0,4},{1,5},{2,6},{3,7},{4,0},{5,1},{6,2},{7,3},{8,12},{9,13},{10,... | collective-permute-start | bytes 159752 | tf_op jit(solution)/shard_map/ppermute | solution.py:294
  20.2 3.9 %collective-permute-done = bf16[208,128]{1,0:T(8,128)(2,1)S(1)} collective-permute-done((bf16[208,128]{1,0:T(8,128)(2,1)S(1)}, bf16[208,128]{1,0:T(8,128)(2,1)S(1)}, u32[]{:S(2)}, u32[]{:S(2)}) %collective-permute-start) | collective-permute-done | bytes 53280 | tf_op jit(solution)/shard_map/ppermute | solution.py:294
  24.1 4.0 %all-to-all-done.1.payload = bf16[8,1,208,128]{3,2,1,0:T(8,128)(2,1)S(1)} async-done(((bf16[8,1,208,128]{3,2,1,0:T(8,128)(2,1)}), bf16[8,1,208,128]{3,2,1,0:T(8,128)(2,1)S(1)}, u32[]{:S(2)}, u32[]{:S(2)}) %all-to-all-start.1) | async-done | bytes 426016 | tf_op jit(solution)/shard_map/all_to_all | solution.py:318
  28.1 0.8 %broadcast_in_dim.2 = bf16[8,1,208,128]{3,2,1,0:T(8,128)(2,1)} broadcast(bf16[208,128]{1,0:T(8,128)(2,1)S(1)} %collective-permute-done), dimensions={2,3} | broadcast | bytes 479232 | tf_op jit(solution)/shard_map/broadcast_in_dim | solution.py:320
  28.9 3.9 %all-to-all-start = ((bf16[8,1,208,128]{3,2,1,0:T(8,128)(2,1)}), bf16[8,1,208,128]{3,2,1,0:T(8,128)(2,1)S(1)}, u32[]{:S(2)}, u32[]{:S(2)}) async-start(bf16[8,1,208,128]{3,2,1,0:T(8,128)(2,1)} %broadcast_in_dim.2), calls=%async_computation | async-start | bytes 851968 | tf_op jit(solution)/shard_map/all_to_all | solution.py:320
  32.8 0.0 copy-done.3
  32.8 0.1 collective-permute-start.1
  32.9 0.0 copy-done.5
  32.9 0.1 copy.11.ranges
  33.0 1.1 %collective-permute-done.1 = s32[1,1024]{1,0:T(1,128)S(1)} collective-permute-done((s32[1,1024]{1,0:T(1,128)S(1)}, s32[1,1024]{1,0:T(1,128)S(1)}, u32[]{:S(2)}, u32[]{:S(2)}) %collective-permute-start.1) | collective-permute-done | bytes 4128 | tf_op jit(solution)/shard_map/ppermute | solution.py:289
  34.0 1.2 %tags.1 = f32[2048,128]{1,0:T(8,128)S(1)} custom-call(s32[32,2]{1,0:T(8,128)S(1)} %copy.11.ranges, s32[8,128]{1,0:T(8,128)S(1)} %bitcast.11, s32[8,128]{1,0:T(8,128)S(1)} %bitcast.12), custom_call_target="tpu_custom_call" | custom-call | flops 131072 | bytes 1048576 | tf_op jit(solution)/shard_map/tags/pallas_call | solution.py:163
  35.2 0.0 collective-permute-done.2.theirs
  35.2 0.0 copy-done
  35.2 2.4 %own_match.1.own_best = f32[2,128]{1,0:T(2,128)S(1)} custom-call(bf16[8,1,208,128]{3,2,1,0:T(8,128)(2,1)S(1)} %all-to-all-done.1.payload, f32[2048,128]{1,0:T(8,128)S(1)} %tags.1, bf16[1024,768]{1,0:T(8,128)(2,1)S(1)} %bitcast.8, bf16[1024,768]{1,0:T(8,128)(2,1)} %collective-permute-done.2.theirs), custom_call_target="tpu_custom_call" | custom-call | flops 805306368 | bytes 3145728 | tf_op jit(solution)/shard_map/own_match/pallas_call | solution.py:329
  37.7 3.0 %all-to-all-done.payload = bf16[8,1,208,128]{3,2,1,0:T(8,128)(2,1)S(1)} async-done(((bf16[8,1,208,128]{3,2,1,0:T(8,128)(2,1)}), bf16[8,1,208,128]{3,2,1,0:T(8,128)(2,1)S(1)}, u32[]{:S(2)}, u32[]{:S(2)}) %all-to-all-start) | async-done | bytes 426016 | tf_op jit(solution)/shard_map/all_to_all | solution.py:320
  40.7 2.4 %cross_match.1 = f32[32,1,128]{2,1,0:T(1,128)S(1)} custom-call(bf16[8,1,208,128]{3,2,1,0:T(8,128)(2,1)S(1)} %all-to-all-done.payload, f32[2048,128]{1,0:T(8,128)S(1)} %tags.1, bf16[1024,768]{1,0:T(8,128)(2,1)S(1)} %bitcast.9, bf16[1024,768]{1,0:T(8,128)(2,1)} %collective-permute-done.2.theirs, f32[2,128]{1,0:T(2,128)S(1)} %own_match.1.own_best), custom_call_target="tpu_custom_call" | custom-call | flops 805306368 | bytes 3145728 | tf_op jit(solution)/shard_map/cross_match/pallas_call | solution.py:338
  43.2 9.5 %all_to_all.15.received = f32[32,1,128]{2,1,0:T(1,128)} all-to-all(f32[32,1,128]{2,1,0:T(1,128)S(1)} %cross_match.1), channel_id=1, replica_groups=mesh['enc'=4,'own'=8] {'enc','own'}, dimensions={0} | all-to-all | bytes 32768 | tf_op jit(solution)/shard_map/all_to_all | solution.py:347
  52.6 1.3 %finish.1 = f32[1,64]{1,0:T(1,128)} custom-call(f32[32,1,128]{2,1,0:T(1,128)} %all_to_all.15.received), custom_call_target="tpu_custom_call" | custom-call | tf_op jit(solution)/shard_map/finish/pallas_call | solution.py:348
Async XLA Ops:
  0.6 34.6 %collective-permute-start.2 = (bf16[1024,768]{1,0:T(8,128)(2,1)}, bf16[1024,768]{1,0:T(8,128)(2,1)}, u32[]{:S(2)}, u32[]{:S(2)}) collective-permute-start(bf16[1024,768]{1,0:T(8,128)(2,1)} %bitcast.7), channel_id=1, source_target_pairs={{0,8},{8,0},{16,24},{24,16},{1,9},{9,1},{17,25},{25,17},{2,10},{10... | collective-permute-start | bytes 4718600 | tf_op jit(solution)/shard_map/ppermute | solution.py:288
  1.9 0.9 %copy-start.1 = (bf16[64,768]{1,0:T(8,128)(2,1)S(1)}, bf16[64,768]{1,0:T(8,128)(2,1)}, u32[]{:S(2)}) copy-start(bf16[64,768]{1,0:T(8,128)(2,1)} %features.1) | copy-start | bytes 294916
  2.8 0.7 %copy-start.2 = (f32[3072]{0:T(1024)S(1)}, f32[3072]{0:T(1024)}, u32[]{:S(2)}) copy-start(f32[3072]{0:T(1024)} %param.13) | copy-start | bytes 36868
  3.5 0.7 %copy-start.4 = (s32[64]{0:T(128)S(1)}, s32[64]{0:T(128)}, u32[]{:S(2)}) copy-start(s32[64]{0:T(128)} %param.10) | copy-start | bytes 772
  4.1 28.6 %copy-start.3 = (s32[1,1024]{1,0:T(1,128)S(1)}, s32[1,1024]{1,0:T(1,128)}, u32[]{:S(2)}) copy-start(s32[1,1024]{1,0:T(1,128)} %param.16) | copy-start | bytes 12292
  4.1 28.7 %copy-start.5 = (s32[32,2]{0,1:T(2,128)S(1)}, s32[32,2]{0,1:T(2,128)}, u32[]{:S(2)}) copy-start(s32[32,2]{0,1:T(2,128)} %param.17) | copy-start | bytes 772
  4.1 31.1 %copy-start = (bf16[1,1024,768]{2,1,0:T(8,128)(2,1)S(1)}, bf16[1,1024,768]{2,1,0:T(8,128)(2,1)}, u32[]{:S(2)}) copy-start(bf16[1,1024,768]{2,1,0:T(8,128)(2,1)} %param.15) | copy-start | bytes 4718596
  11.8 16.3 %all-to-all-start.1 = ((bf16[8,1,208,128]{3,2,1,0:T(8,128)(2,1)}), bf16[8,1,208,128]{3,2,1,0:T(8,128)(2,1)S(1)}, u32[]{:S(2)}, u32[]{:S(2)}) async-start(bf16[8,1,208,128]{3,2,1,0:T(8,128)(2,1)} %get-tuple-element.7), calls=%async_computation.1 | async-start | bytes 851968 | tf_op jit(solution)/shard_map/all_to_all | solution.py:318
  17.6 6.5 %collective-permute-start = (bf16[208,128]{1,0:T(8,128)(2,1)S(1)}, bf16[208,128]{1,0:T(8,128)(2,1)S(1)}, u32[]{:S(2)}, u32[]{:S(2)}) collective-permute-start(bf16[208,128]{1,0:T(8,128)(2,1)S(1)} %bitcast.14), channel_id=1, source_target_pairs={{0,4},{1,5},{2,6},{3,7},{4,0},{5,1},{6,2},{7,3},{8,12},{9,13},{10,... | collective-permute-start | bytes 159752 | tf_op jit(solution)/shard_map/ppermute | solution.py:294
  28.9 11.8 %all-to-all-start = ((bf16[8,1,208,128]{3,2,1,0:T(8,128)(2,1)}), bf16[8,1,208,128]{3,2,1,0:T(8,128)(2,1)S(1)}, u32[]{:S(2)}, u32[]{:S(2)}) async-start(bf16[8,1,208,128]{3,2,1,0:T(8,128)(2,1)} %broadcast_in_dim.2), calls=%async_computation | async-start | bytes 851968 | tf_op jit(solution)/shard_map/all_to_all | solution.py:320
  32.8 1.2 %collective-permute-start.1 = (s32[1,1024]{1,0:T(1,128)S(1)}, s32[1,1024]{1,0:T(1,128)S(1)}, u32[]{:S(2)}, u32[]{:S(2)}) collective-permute-start(s32[1,1024]{1,0:T(1,128)S(1)} %copy-done.3), channel_id=1, source_target_pairs={{0,8},{8,0},{16,24},{24,16},{1,9},{9,1},{17,25},{25,17},{2,10},{10... | collective-permute-start | bytes 12296 | tf_op jit(solution)/shard_map/ppermute | solution.py:289

commit v2 on v1

v2 whole, which is shorter than its diff:
```python
import functools
import math

import jax
import jax.numpy as jnp
from jax import lax
from jax.experimental import pallas as pl
from jax.experimental.pallas import tpu as pltpu
from jax.sharding import PartitionSpec as P

lowest_score = -1e30
quad = 4
lanes = 128
pad_rows = 16


def whole_spec(space=pltpu.VMEM):
    return pl.BlockSpec(memory_space=space)


def from_hbm(value):
    return pltpu.with_memory_space_constraint(value, pltpu.HBM)


def flat(value):
    return len(value.shape) == 1


def stage_kernel(*refs):
    count = (len(refs) - 1) // 2
    sems = refs[-1]
    copies = [
        pltpu.make_async_copy(refs[index], refs[count + index].at[0] if flat(refs[index]) else refs[count + index], sems.at[index])
        for index in range(count)
    ]
    for copy in copies:
        copy.start()
    for copy in copies:
        copy.wait()


def stage(*values):
    return pl.pallas_call(
        stage_kernel,
        in_specs=[whole_spec(pl.ANY)] * len(values),
        out_specs=[whole_spec()] * len(values),
        out_shape=[
            jax.ShapeDtypeStruct((1,) * flat(value) + value.shape, value.dtype) for value in values
        ],
        scratch_shapes=[pltpu.SemaphoreType.DMA((len(values),))],
        cost_estimate=pl.CostEstimate(
            flops=0,
            bytes_accessed=2 * sum(value.size * value.dtype.itemsize for value in values),
            transcendentals=0,
        ),
        compiler_params=pltpu.CompilerParams(vmem_limit_bytes=16 << 20),
        name="stage",
    )(*[from_hbm(value) for value in values])


def split_kernel(groups, features, labels, out, columns):
    docs, width = features.shape
    per = docs // groups
    blocks = width // lanes
    group = lax.axis_index("own") // quad
    for block in range(blocks):
        columns[block] = features[:, block * lanes : (block + 1) * lanes].astype(jnp.float32)
    rows = jnp.broadcast_to(labels[...].astype(jnp.float32), (pad_rows, docs)).astype(jnp.bfloat16)
    for shift in range(1, groups):
        residue = lax.rem(group + shift, groups)
        for block in range(blocks):
            out[shift - 1, pl.ds(block * per, per), :] = residue_rows(
                columns, block, groups, per, residue
            )
        out[shift - 1, pl.ds(blocks * per, pad_rows), :] = residue_tags(rows, groups, per, residue)


def residue_rows(columns, block, groups, per, residue):
    piece = columns[block, pl.ds(0, per, stride=groups), :]
    for choice in range(1, groups):
        piece = jnp.where(
            residue == choice, columns[block, pl.ds(choice, per, stride=groups), :], piece
        )
    return piece.astype(jnp.bfloat16)


def residue_tags(rows, groups, per, residue):
    docs = rows.shape[1]
    source = lax.broadcasted_iota(jnp.int32, (docs, lanes), 0)
    column = lax.broadcasted_iota(jnp.int32, (docs, lanes), 1)
    pick = (source == (column % per) * groups + residue).astype(jnp.bfloat16)
    return jnp.dot(rows, pick, preferred_element_type=jnp.float32).astype(jnp.bfloat16)


def split(features, labels, groups):
    docs, width = features.shape
    rows = width // lanes * (docs // groups) + pad_rows
    return pl.pallas_call(
        functools.partial(split_kernel, groups),
        in_specs=[whole_spec()] * 2,
        out_specs=whole_spec(),
        out_shape=jax.ShapeDtypeStruct((groups - 1, rows, lanes), jnp.bfloat16),
        scratch_shapes=[pltpu.VMEM((width // lanes, docs, lanes), jnp.float32)],
        compiler_params=pltpu.CompilerParams(vmem_limit_bytes=4 << 20),
        name="split",
    )(from_hbm(features), from_hbm(labels))


def encode_kernel(
    groups,
    features,
    labels,
    arrived,
    gain,
    w_in,
    b_in,
    w_out,
    embeddings,
    payload,
    normed,
    columns,
):
    docs, width = features.shape
    hidden = w_in.shape[1]
    per = docs // groups
    blocks = width // lanes
    chunk = 512 if hidden % 512 == 0 else hidden
    inputs = jnp.concatenate(
        [features[...].astype(jnp.float32)]
        + [
            jnp.concatenate(
                [
                    arrived[slot, pl.ds(block * per, per), :].astype(jnp.float32)
                    for block in range(blocks)
                ],
                axis=1,
            )
            for slot in range(groups - 1)
        ],
        axis=0,
    )
    center = inputs - jnp.mean(inputs, axis=1, keepdims=True)
    spread = jnp.mean(center * center, axis=1, keepdims=True)
    normed[...] = (center * lax.rsqrt(spread + 1e-05) * gain[...]).astype(jnp.bfloat16)
    output = inputs
    waiting = None
    for start in range(0, hidden + chunk, chunk):
        raised = None
        if start < hidden:
            raised = (
                jnp.dot(
                    normed[...], w_in[:, pl.ds(start, chunk)], preferred_element_type=jnp.float32
                )
                + b_in[:, pl.ds(start, chunk)]
            )
        if waiting is not None:
            middle = jax.nn.gelu(waiting, approximate=True).astype(jnp.bfloat16)
            output = output + jnp.dot(
                middle, w_out[pl.ds(start - chunk, chunk), :], preferred_element_type=jnp.float32
            )
        waiting = raised
    scaled = output * lax.rsqrt(jnp.mean(output * output, axis=1, keepdims=True) + 1e-06)
    embeddings[...] = scaled[0:docs].astype(jnp.bfloat16)
    group = lax.axis_index("own") // quad
    tags = residue_tags(
        jnp.broadcast_to(labels[...].astype(jnp.float32), (pad_rows, docs)).astype(jnp.bfloat16),
        groups,
        per,
        group,
    )
    column = lax.broadcasted_iota(jnp.int32, (pad_rows, lanes), 1) % docs // per
    for slot in range(1, groups):
        tags = jnp.where(
            column == slot, arrived[slot - 1, pl.ds(blocks * per, pad_rows), :], tags
        )
    for block in range(blocks):
        columns[block] = scaled[0:docs, block * lanes : (block + 1) * lanes]
        pieces = [residue_rows(columns, block, groups, per, group)] + [
            scaled[
                docs + slot * per : docs + (slot + 1) * per, block * lanes : (block + 1) * lanes
            ].astype(jnp.bfloat16)
            for slot in range(groups - 1)
        ]
        for slot in range(groups):
            payload[pl.ds(block * docs + slot * per, per), :] = pieces[slot]
    payload[pl.ds(blocks * docs, pad_rows), :] = tags


def encode(features, labels, arrived, norm_gain, w_in, b_in, w_out, groups):
    docs, width = features.shape
    hidden = w_in.shape[1]
    per = docs // groups
    total = docs + (groups - 1) * per
    rows = width // lanes * docs + pad_rows
    return pl.pallas_call(
        functools.partial(encode_kernel, groups),
        in_specs=[whole_spec()] * 7,
        out_specs=[whole_spec()] * 2,
        out_shape=[
            jax.ShapeDtypeStruct((docs, width), jnp.bfloat16),
            jax.ShapeDtypeStruct((rows, lanes), jnp.bfloat16),
        ],
        scratch_shapes=[
            pltpu.VMEM((total, width), jnp.bfloat16),
            pltpu.VMEM((width // lanes, docs, lanes), jnp.float32),
        ],
        cost_estimate=pl.CostEstimate(
            flops=4 * total * width * hidden,
            bytes_accessed=4 * width * hidden,
            transcendentals=total * hidden,
        ),
        compiler_params=pltpu.CompilerParams(vmem_limit_bytes=20 << 20),
        name="encode",
    )(
        features,
        labels,
        arrived,
        norm_gain,
        w_in,
        b_in,
        w_out,
    )


def tags_kernel(ranges, mine, theirs, store, out, held_store, sem):
    copy = pltpu.make_async_copy(store, held_store, sem)
    copy.start()
    owner = lax.axis_index("own")
    clusters = ranges.shape[0]
    held = []
    for labels in (mine, theirs):
        value = labels[...]
        inside = jnp.zeros(value.shape, jnp.bool_)
        for cluster in range(clusters):
            spans = (ranges[cluster, 0] <= owner) & (owner <= ranges[cluster, 1])
            inside = inside | (value == jnp.where(spans, cluster, -2))
        held.append(jnp.where(inside, value, -1).astype(jnp.float32))
    flat_tags = jnp.concatenate(held, axis=0)
    lines = flat_tags.shape[0]
    square = jnp.concatenate(
        [flat_tags, jnp.zeros((lanes - lines, lanes), jnp.float32)], axis=0
    ).T
    for line in range(lines):
        out[pl.ds(line * lanes, lanes), :] = jnp.broadcast_to(
            square[:, line : line + 1], (lanes, lanes)
        )
    copy.wait()


def member_tags(cluster_range, mine, theirs, store):
    total = mine.size
    return pl.pallas_call(
        tags_kernel,
        in_specs=[whole_spec(pltpu.SMEM), whole_spec(), whole_spec(), whole_spec(pl.ANY)],
        out_specs=[whole_spec()] * 2,
        out_shape=[
            jax.ShapeDtypeStruct((2 * total, lanes), jnp.float32),
            jax.ShapeDtypeStruct(store.shape, store.dtype),
        ],
        scratch_shapes=[pltpu.SemaphoreType.DMA],
        cost_estimate=pl.CostEstimate(
            flops=total * lanes, bytes_accessed=8 * total * lanes, transcendentals=0
        ),
        compiler_params=pltpu.CompilerParams(vmem_limit_bytes=4 << 20),
        name="tags",
    )(
        cluster_range,
        mine.reshape(-1, lanes),
        theirs.reshape(-1, lanes),
        from_hbm(store),
    )


def partner(place, step, peers):
    if peers & (peers - 1) == 0:
        return place ^ step
    return (place + peers - step) % peers


def back(place, step, peers):
    if peers & (peers - 1) == 0:
        return place ^ step
    return (place + step) % peers


def best_rows(docs, chunks, tags, stores):
    blocks = stores[0].shape[1] // lanes
    pair = lanes // docs
    rows = jnp.concatenate(
        [
            jnp.concatenate([chunk[pl.ds(block * docs, docs), :] for chunk in chunks], axis=0)
            for block in range(blocks)
        ],
        axis=1,
    )
    column = lax.broadcasted_iota(jnp.int32, (1, lanes), 1) // docs
    wanted = []
    for first in range(0, len(chunks), pair):
        row = jnp.zeros((1, lanes), jnp.float32)
        for part in range(pair):
            held = chunks[first + part][pl.ds(blocks * docs, pad_rows), :]
            row = jnp.where(column == part, held[0:1].astype(jnp.float32), row)
        wanted.append(row)
    best = [jnp.full((8, lanes), lowest_score, jnp.float32) for unused in wanted]
    tall = 256
    first = 0
    for store in stores:
        for start in range(0, store.shape[0], tall):
            score = lax.dot_general(
                store[pl.ds(start, tall), :],
                rows,
                (((1,), (1,)), ((), ())),
                preferred_element_type=jnp.float32,
            )
            held = tags[pl.ds(first, tall), :]
            first += tall
            for index, row in enumerate(wanted):
                piece = jnp.where(
                    held == row, score[:, index * lanes : (index + 1) * lanes], lowest_score
                )
                best[index] = jnp.maximum(
                    best[index], jnp.max(piece.reshape(tall // 8, 8, lanes), axis=0)
                )
    return [jnp.max(piece, axis=0, keepdims=True) for piece in best]


def early_kernel(docs, tags, mine, theirs, *refs):
    out = refs[-1]
    for index, row in enumerate(best_rows(docs, refs[:-1], tags, (mine, theirs))):
        out[pl.ds(index, 1), :] = row


def late_kernel(groups, owners, docs, peers, tags, mine, theirs, early, *refs):
    out = refs[-1]
    pair = lanes // docs
    rows = [early[pl.ds(index, 1), :] for index in range(early.shape[0])]
    rows = rows + best_rows(docs, refs[:-1], tags, (mine, theirs))
    encoder = lax.axis_index("enc")
    owner = lax.axis_index("own")
    core = lax.rem(encoder, 2)
    group = owner // quad
    place = encoder // 2 * quad + lax.rem(owner, quad)
    out[...] = jnp.zeros(out.shape, out.dtype)
    for slot, step in enumerate(steps_of(peers)):
        home = partner(place, step, peers)
        for shift in range(groups):
            origin = lax.rem(group + groups - shift, groups)
            target = (2 * (home // quad) + core) * owners + origin * quad + lax.rem(home, quad)
            out[target] = rows[slot // pair]


def steps_of(peers):
    def order(step):
        bits = bin(step).count("1")
        return (bits > 0, bits > 1, -bits, step)

    return sorted(range(peers), key=order)


def finish_kernel(groups, owners, per, scale, received, out):
    docs = out.shape[1]
    peers = received.shape[0] // (2 * groups)
    pair = lanes // docs
    encoder = lax.axis_index("enc")
    owner = lax.axis_index("own")
    core = lax.rem(encoder, 2)
    group = owner // quad
    place = (encoder // 2) * quad + lax.rem(owner, quad)
    column = lax.broadcasted_iota(jnp.int32, (8, lanes), 1)
    result = jnp.full((8, lanes), lowest_score, jnp.float32)
    for source in range(groups):
        shift = lax.rem(source + groups - group, groups)
        for part in range(pair):
            best = jnp.full((1, lanes), lowest_score, jnp.float32)
            for slot, step in enumerate(steps_of(peers)):
                if slot % pair == part:
                    sender = back(place, step, peers)
                    row = (2 * (sender // quad) + core) * owners + source * quad
                    best = jnp.maximum(best, received[row + lax.rem(sender, quad)])
            index = lax.rem(part * docs + shift * per + column // groups, lanes)
            taken = jnp.take_along_axis(jnp.broadcast_to(best, (8, lanes)), index, axis=1)
            result = jnp.where(column % groups == source, jnp.maximum(result, taken), result)
    out[...] = (result * scale)[0:1, 0:docs]


def program(
    features, doc_cluster, norm_gain, w_in, b_in, w_out, members, member_cluster, cluster_range
):
    owners = lax.axis_size("own")
    encoders = lax.axis_size("enc")
    docs, width = features.shape
    groups = owners // quad
    per = docs // groups
    peers = encoders // 2 * quad
    axes = ("enc", "own")
    swap = [(index, index ^ 1) for index in range(encoders)]
    mine = members.reshape(-1, width)
    labels = doc_cluster.reshape(1, docs)
    leaving = split(features, labels, groups)
    arrived = []
    for shift in range(1, groups):
        arrived.append(
            lax.ppermute(
                leaving[shift - 1],
                "own",
                [(index, (index + quad * shift) % owners) for index in range(owners)],
            )
        )
    theirs = lax.ppermute(mine, "enc", swap)
    their_labels = lax.ppermute(member_cluster, "enc", swap)
    staged = stage(
        w_in,
        w_out,
        b_in.reshape(1, -1),
        norm_gain,
        features,
        labels,
    )
    w_in, w_out, b_in, norm_gain, features, labels = staged
    embeddings, payload = encode(
        features, labels, jnp.stack(arrived), norm_gain, w_in, b_in, w_out, groups
    )
    tags, theirs = member_tags(cluster_range, member_cluster, their_labels, theirs)
    chunks = []
    for step in steps_of(peers):
        route = []
        for index in range(encoders * owners):
            encoder, owner = divmod(index, owners)
            place = encoder // 2 * quad + owner % quad
            target = back(place, step, peers)
            route.append(
                (
                    index,
                    (2 * (target // quad) + encoder % 2) * owners
                    + owner // quad * quad
                    + target % quad,
                )
            )
        chunks.append(lax.ppermute(payload, axes, route) if step else payload)
    half = peers // 2
    cost = pl.CostEstimate(
        flops=2 * peers * docs * mine.shape[0] * width,
        bytes_accessed=4 * mine.shape[0] * width,
        transcendentals=0,
    )
    params = pltpu.CompilerParams(vmem_limit_bytes=10 << 20)
    early = pl.pallas_call(
        functools.partial(early_kernel, docs),
        in_specs=[whole_spec()] * (3 + half),
        out_specs=whole_spec(),
        out_shape=jax.ShapeDtypeStruct((half * docs // lanes, lanes), jnp.float32),
        cost_estimate=cost,
        compiler_params=params,
        name="early_match",
    )(tags, mine, theirs, *chunks[:half])
    replies = pl.pallas_call(
        functools.partial(late_kernel, groups, owners, docs, peers),
        in_specs=[whole_spec()] * (4 + peers - half),
        out_specs=whole_spec(),
        out_shape=jax.ShapeDtypeStruct((encoders * owners, 1, lanes), jnp.float32),
        cost_estimate=cost,
        compiler_params=params,
        name="late_match",
    )(tags, mine, theirs, early, *chunks[half:])
    received = lax.all_to_all(replies, axes, split_axis=0, concat_axis=0, tiled=True)
    maxsim = pl.pallas_call(
        functools.partial(finish_kernel, groups, owners, per, 1.0 / math.sqrt(width)),
        in_specs=[whole_spec()],
        out_specs=whole_spec(),
        out_shape=jax.ShapeDtypeStruct((1, docs), jnp.float32),
        name="finish",
    )(received)
    return (embeddings, maxsim.reshape(docs))


def solution(mesh):
    placed = (
        P(("enc", "own"), None),
        P(("enc", "own")),
        P(),
        P(),
        P(),
        P(),
        P("own", "enc", None),
        P("own", "enc"),
        P(),
    )
    return jax.shard_map(
        program,
        mesh=mesh,
        in_specs=placed,
        out_specs=(P(("enc", "own"), None), P(("enc", "own"))),
        check_vma=False,
    )
```

time: 54.5 us -> 42.9 us (0.79)
  waiting for transfers between devices: 12 us -> 4.33 us
  local copies, waits for them, and re-layouts: 3.85 us -> 1.28 us
  Pallas kernels: 15.1 us -> 13.2 us
  starting transfers between devices: 12.8 us -> 13.5 us
    ppermute x3 -> x10, starting transfers between devices: 3.22 us -> 13.5 us  [the longest x7 9.34 us: program(): chunks.append(lax.ppermute(payload, axes, route) if step else payload)]
    all_to_all x2 -> x0, starting transfers between devices: 9.61 us -> none  [the longest x1 5.74 us: shards(): own_all = spread(own_rows)]
    all_to_all x2 -> x0, waiting for transfers between devices: 7.04 us -> none  [the longest x1 4 us: shards(): own_all = spread(own_rows)]
    pallas_call x4 -> x6, Pallas kernels: 13.9 us -> 10.9 us  [the longest x1 3.83 us: stage(): pl.pallas_call(stage_kernel, in_specs=[whole_spec(pl.ANY)] * len(values),...]
    pallas_call x1, Pallas kernels: 1.19 us -> 2.28 us  [member_tags(): pl.pallas_call(tags_kernel, in_specs=[whole_spec(pltpu.SMEM), whole_spec(...]
    unnamed x13 -> x9, local copies, waits for them, and re-layouts: 2.35 us -> 1.28 us
    broadcast_in_dim x1 -> x0, local copies, waits for them, and re-layouts: 0.81 us -> none  [shards(): jnp.broadcast_to(stacked[None], (peers,) + stacked.shape)]
    reshape x1 -> x0, local copies, waits for them, and re-layouts: 0.69 us -> none  [encode(): norm_gain.reshape(1, width)]
  transfers between devices with their start and end apart: 5 -> 10, of which waited for: 4 -> 3; matrix products, arithmetic and copies ran while one was open for 3% -> 0% of each run, Pallas kernels for 21% -> 25%
where the time goes in v2:
time: 42.9 us; the launch traced here: 42.7 us
  starting transfers between devices  13.5 us (31%)
  Pallas kernels  13.2 us (31%)
  blocking collectives  9.69 us (23%)
  waiting for transfers between devices  4.33 us (10%)
  local copies, waits for them, and re-layouts  1.28 us (3%)
  between operations  0.73 us (2%)
    all_to_all x1, blocking collectives, program(): lax.all_to_all(replies, axes, split_axis=0, concat_axis=0, tiled=True)  9.69 us
    ppermute x7, starting transfers between devices, program(): chunks.append(lax.ppermute(payload, axes, route) if step else payload)  9.34 us
    pallas_call x1, Pallas kernels, stage(): pl.pallas_call(stage_kernel, in_specs=[whole_spec(pl.ANY)] * len(values),...  3.83 us
    ppermute x1, starting transfers between devices, program(): lax.ppermute(leaving[shift - 1], 'own', [(index, (index + quad * shift) %...  3.59 us
    ppermute x7, waiting for transfers between devices, program(): chunks.append(lax.ppermute(payload, axes, route) if step else payload)  3.16 us
    pallas_call x1, Pallas kernels, encode(): pl.pallas_call(functools.partial(encode_kernel, groups), in_specs=[whole_...  2.56 us
    pallas_call x1, Pallas kernels, member_tags(): pl.pallas_call(tags_kernel, in_specs=[whole_spec(pltpu.SMEM), whole_spec(...  2.28 us
    pallas_call x1, Pallas kernels, program(): pl.pallas_call(functools.partial(finish_kernel, groups, owners, per, 1.0...  1.36 us
  transfers between devices with their start and end apart: 10, of which 3 were waited for; matrix products, arithmetic and copies ran while one was open for 0% of the time, Pallas kernels for 25%

profile of v2, /device:TPU:0, one launch (start us, length us, event | category | flops | bytes accessed | tf_op | source)
XLA Modules:
  0.0 42.7 jit_solution(2342986223181668837)
XLA Ops:
  0.6 0.6 %collective-permute-start.2 = (bf16[1024,768]{1,0:T(8,128)(2,1)}, bf16[1024,768]{1,0:T(8,128)(2,1)S(1)}, u32[]{:S(2)}, u32[]{:S(2)}) collective-permute-start(bf16[1024,768]{1,0:T(8,128)(2,1)} %bitcast.8), channel_id=1, source_target_pairs={{0,8},{8,0},{16,24},{24,16},{1,9},{9,1},{17,25},{25,17},{2,10},{10... | collective-permute-start | bytes 4718600 | tf_op jit(solution)/shard_map/ppermute | solution.py:409
  1.2 1.0 %split.1 = bf16[1,208,128]{2,1,0:T(8,128)(2,1)S(1)} custom-call(bf16[64,768]{1,0:T(8,128)(2,1)} %features.1, s32[1,64]{1,0:T(1,128)} %bitcast.16), custom_call_target="tpu_custom_call" | custom-call | tf_op jit(solution)/shard_map/split/pallas_call | solution.py:98
  2.2 3.6 %collective-permute-start = (bf16[208,128]{1,0:T(8,128)(2,1)S(1)}, bf16[208,128]{1,0:T(8,128)(2,1)S(1)}, u32[]{:S(2)}, u32[]{:S(2)}) collective-permute-start(bf16[208,128]{1,0:T(8,128)(2,1)S(1)} %bitcast.12), channel_id=1, source_target_pairs={{0,4},{1,5},{2,6},{3,7},{4,0},{5,1},{6,2},{7,3},{8,12},{9,13},{10,... | collective-permute-start | bytes 159752 | tf_op jit(solution)/shard_map/ppermute | solution.py:403
  5.8 3.8 %stage.1 = (bf16[768,3072]{1,0:T(8,128)(2,1)S(1)}, bf16[3072,768]{1,0:T(8,128)(2,1)S(1)}, f32[1,3072]{1,0:T(1,128)S(1)}, f32[1,768]{1,0:T(1,128)S(1)}, bf16[64,768]{1,0:T(8,128)(2,1)S(1)}, /*index=5*/s32[1,64]{1,0:T(1,128)S(1)}) custom-call(bf16[768,3072]{1,0:T(8,128)(2,1)} %refs_0_.1, bf16[3072,768]{1,0:T(8,128)(2,1)} %refs_1_.1, f32[1,3072]{1,0:T(1,128)} %bitcast.15, ...), custom_call_target="tpu_custom_call" | custom-call | bytes 19102208 | tf_op jit(solution)/shard_map/stage/pallas_call | solution.py:43
  9.7 0.0 collective-permute-done
  9.7 0.0 copy-start.1
  9.7 0.0 copy-start.3
  9.7 0.0 copy-start
  9.7 2.6 %encode.1 = (bf16[64,768]{1,0:T(8,128)(2,1)}, bf16[400,128]{1,0:T(8,128)(2,1)S(1)}) custom-call(bf16[64,768]{1,0:T(8,128)(2,1)S(1)} %get-tuple-element.12.features, s32[1,64]{1,0:T(1,128)S(1)} %get-tuple-element.13.labels, bf16[1,208,128]{2,1,0:T(8,128)(2,1)S(1)} %bitcast.11, f32[1,768]{1,0:T(1,128)S(1)} %get-tuple-element.14.gain, ...), custom_call_target="tpu_custom_call" | custom-call | flops 905969664 | bytes 9437184 | tf_op jit(solution)/shard_map/encode/pallas_call | solution.py:195
  12.3 1.5 %collective-permute-start.3 = (bf16[400,128]{1,0:T(8,128)(2,1)S(1)}, bf16[400,128]{1,0:T(8,128)(2,1)S(1)}, u32[]{:S(2)}, u32[]{:S(2)}) collective-permute-start(bf16[400,128]{1,0:T(8,128)(2,1)S(1)} %get-tuple-element.21.refs_0_), channel_id=1, source_target_pairs={{0,1},{1,0},{2,3},{3,2},{4,5},{5,4},{6,7},{7,6},{8,9},{9,8},{10,11... | collective-permute-start | bytes 307208 | tf_op jit(solution)/shard_map/ppermute | solution.py:439
  13.8 1.6 %collective-permute-start.4 = (bf16[400,128]{1,0:T(8,128)(2,1)S(1)}, bf16[400,128]{1,0:T(8,128)(2,1)S(1)}, u32[]{:S(2)}, u32[]{:S(2)}) collective-permute-start(bf16[400,128]{1,0:T(8,128)(2,1)S(1)} %get-tuple-element.21.refs_0_), channel_id=1, source_target_pairs={{0,2},{1,3},{2,0},{3,1},{4,6},{5,7},{6,4},{7,5},{8,10},{9,11},{10,... | collective-permute-start | bytes 307208 | tf_op jit(solution)/shard_map/ppermute | solution.py:439
  15.4 1.5 %collective-permute-start.5 = (bf16[400,128]{1,0:T(8,128)(2,1)S(1)}, bf16[400,128]{1,0:T(8,128)(2,1)S(1)}, u32[]{:S(2)}, u32[]{:S(2)}) collective-permute-start(bf16[400,128]{1,0:T(8,128)(2,1)S(1)} %get-tuple-element.21.refs_0_), channel_id=1, source_target_pairs={{0,16},{1,17},{2,18},{3,19},{4,20},{5,21},{6,22},{7,23},{8,24},{9,... | collective-permute-start | bytes 307208 | tf_op jit(solution)/shard_map/ppermute | solution.py:439
  16.9 0.0 copy-done.1
  16.9 0.0 collective-permute-start.1
  16.9 1.2 %collective-permute-done.1 = s32[1,1024]{1,0:T(1,128)S(1)} collective-permute-done((s32[1,1024]{1,0:T(1,128)S(1)}, s32[1,1024]{1,0:T(1,128)S(1)}, u32[]{:S(2)}, u32[]{:S(2)}) %collective-permute-start.1) | collective-permute-done | bytes 4128 | tf_op jit(solution)/shard_map/ppermute | solution.py:410
  18.0 0.4 collective-permute-start.6
  18.4 0.0 collective-permute-done.3.refs_1_
  18.4 2.5 %collective-permute-start.7 = (bf16[400,128]{1,0:T(8,128)(2,1)S(1)}, bf16[400,128]{1,0:T(8,128)(2,1)S(1)}, u32[]{:S(2)}, u32[]{:S(2)}) collective-permute-start(bf16[400,128]{1,0:T(8,128)(2,1)S(1)} %get-tuple-element.21.refs_0_), channel_id=1, source_target_pairs={{0,3},{1,2},{2,1},{3,0},{4,7},{5,6},{6,5},{7,4},{8,11},{9,10},{10,... | collective-permute-start | bytes 307208 | tf_op jit(solution)/shard_map/ppermute | solution.py:439
  20.9 0.0 collective-permute-done.4.refs_2_
  20.9 1.4 %collective-permute-start.8 = (bf16[400,128]{1,0:T(8,128)(2,1)S(1)}, bf16[400,128]{1,0:T(8,128)(2,1)S(1)}, u32[]{:S(2)}, u32[]{:S(2)}) collective-permute-start(bf16[400,128]{1,0:T(8,128)(2,1)S(1)} %get-tuple-element.21.refs_0_), channel_id=1, source_target_pairs={{0,17},{1,16},{2,19},{3,18},{4,21},{5,20},{6,23},{7,22},{8,25},{9,... | collective-permute-start | bytes 307208 | tf_op jit(solution)/shard_map/ppermute | solution.py:439
  22.4 0.0 collective-permute-done.2.store
  22.4 0.0 copy-start.2
  22.4 1.2 %copy-done.2 = bf16[1024,768]{1,0:T(8,128)(2,1)} copy-done((bf16[1024,768]{1,0:T(8,128)(2,1)}, bf16[1024,768]{1,0:T(8,128)(2,1)S(1)}, u32[]{:S(2)}) %copy-start.2) | copy-done | bytes 1572888
  23.5 0.4 collective-permute-start.9
  24.0 0.0 copy-done.3
  24.0 0.1 copy.11.ranges
  24.1 2.3 %tags.1 = (f32[2048,128]{1,0:T(8,128)S(1)}, bf16[1024,768]{1,0:T(8,128)(2,1)S(1)}) custom-call(s32[32,2]{1,0:T(8,128)S(1)} %copy.11.ranges, s32[8,128]{1,0:T(8,128)S(1)} %bitcast.13, s32[8,128]{1,0:T(8,128)S(1)} %bitcast.14, bf16[1024,768]{1,0:T(8,128)(2,1)} %copy-done.2), custom_call_target="tpu_custom_call" | custom-call | flops 131072 | bytes 1048576 | tf_op jit(solution)/shard_map/tags/pallas_call | solution.py:252
  26.3 0.0 collective-permute-done.5.refs_3_
  26.4 0.0 copy-done
  26.4 1.0 %early_match.1.early = f32[2,128]{1,0:T(2,128)S(1)} custom-call(f32[2048,128]{1,0:T(8,128)S(1)} %get-tuple-element.19.tags, bf16[1024,768]{1,0:T(8,128)(2,1)S(1)} %bitcast.9, bf16[1024,768]{1,0:T(8,128)(2,1)S(1)} %get-tuple-element.20.theirs, bf16[400,128]{1,0:T(8,128)(2,1)S(1)} %get-tuple-element.21.refs_0_, ...), custom_call_target="tpu_custom_call" | custom-call | flops 805306368 | bytes 3145728 | tf_op jit(solution)/shard_map/early_match/pallas_call | solution.py:447
  27.4 0.0 collective-permute-done.6.refs_0_
  27.4 0.5 %collective-permute-done.7.refs_1_ = bf16[400,128]{1,0:T(8,128)(2,1)S(1)} collective-permute-done((bf16[400,128]{1,0:T(8,128)(2,1)S(1)}, bf16[400,128]{1,0:T(8,128)(2,1)S(1)}, u32[]{:S(2)}, u32[]{:S(2)}) %collective-permute-start.7) | collective-permute-done | bytes 102432 | tf_op jit(solution)/shard_map/ppermute | solution.py:439
  28.0 2.6 %collective-permute-done.8.refs_2_ = bf16[400,128]{1,0:T(8,128)(2,1)S(1)} collective-permute-done((bf16[400,128]{1,0:T(8,128)(2,1)S(1)}, bf16[400,128]{1,0:T(8,128)(2,1)S(1)}, u32[]{:S(2)}, u32[]{:S(2)}) %collective-permute-start.8) | collective-permute-done | bytes 102432 | tf_op jit(solution)/shard_map/ppermute | solution.py:439
  30.6 0.0 collective-permute-done.9.refs_3_
  30.6 1.1 %late_match.1 = f32[32,1,128]{2,1,0:T(1,128)S(1)} custom-call(f32[2048,128]{1,0:T(8,128)S(1)} %get-tuple-element.19.tags, bf16[1024,768]{1,0:T(8,128)(2,1)S(1)} %bitcast.10, bf16[1024,768]{1,0:T(8,128)(2,1)S(1)} %get-tuple-element.20.theirs, f32[2,128]{1,0:T(2,128)S(1)} %early_match.1.early, bf16[400,128]{1,0:T(8,128)(2,1)S(1)} %collective-permute-done.6.refs_0_, ...), custom_call_target="tpu_custom_call" | custom-call | flops 805306368 | bytes 3145728 | tf_op jit(solution)/shard_map/late_match/pallas_call | solution.py:456
  31.6 9.7 %all_to_all.5.received = f32[32,1,128]{2,1,0:T(1,128)} all-to-all(f32[32,1,128]{2,1,0:T(1,128)S(1)} %late_match.1), channel_id=1, replica_groups=mesh['enc'=4,'own'=8] {'enc','own'}, dimensions={0} | all-to-all | bytes 32768 | tf_op jit(solution)/shard_map/all_to_all | solution.py:465
  41.3 1.4 %finish.1 = f32[1,64]{1,0:T(1,128)} custom-call(f32[32,1,128]{2,1,0:T(1,128)} %all_to_all.5.received), custom_call_target="tpu_custom_call" | custom-call | tf_op jit(solution)/shard_map/finish/pallas_call | solution.py:466
Async XLA Ops:
  0.6 21.7 %collective-permute-start.2 = (bf16[1024,768]{1,0:T(8,128)(2,1)}, bf16[1024,768]{1,0:T(8,128)(2,1)S(1)}, u32[]{:S(2)}, u32[]{:S(2)}) collective-permute-start(bf16[1024,768]{1,0:T(8,128)(2,1)} %bitcast.8), channel_id=1, source_target_pairs={{0,8},{8,0},{16,24},{24,16},{1,9},{9,1},{17,25},{25,17},{2,10},{10... | collective-permute-start | bytes 4718600 | tf_op jit(solution)/shard_map/ppermute | solution.py:409
  2.2 7.4 %collective-permute-start = (bf16[208,128]{1,0:T(8,128)(2,1)S(1)}, bf16[208,128]{1,0:T(8,128)(2,1)S(1)}, u32[]{:S(2)}, u32[]{:S(2)}) collective-permute-start(bf16[208,128]{1,0:T(8,128)(2,1)S(1)} %bitcast.12), channel_id=1, source_target_pairs={{0,4},{1,5},{2,6},{3,7},{4,0},{5,1},{6,2},{7,3},{8,12},{9,13},{10,... | collective-permute-start | bytes 159752 | tf_op jit(solution)/shard_map/ppermute | solution.py:403
  9.7 7.2 %copy-start.1 = (s32[1,1024]{1,0:T(1,128)S(1)}, s32[1,1024]{1,0:T(1,128)}, u32[]{:S(2)}) copy-start(s32[1,1024]{1,0:T(1,128)} %param.16) | copy-start | bytes 12292
  9.7 14.3 %copy-start.3 = (s32[32,2]{0,1:T(2,128)S(1)}, s32[32,2]{0,1:T(2,128)}, u32[]{:S(2)}) copy-start(s32[32,2]{0,1:T(2,128)} %param.17) | copy-start | bytes 772
  9.7 16.7 %copy-start = (bf16[1,1024,768]{2,1,0:T(8,128)(2,1)S(1)}, bf16[1,1024,768]{2,1,0:T(8,128)(2,1)}, u32[]{:S(2)}) copy-start(bf16[1,1024,768]{2,1,0:T(8,128)(2,1)} %param.15) | copy-start | bytes 4718596
  12.3 6.1 %collective-permute-start.3 = (bf16[400,128]{1,0:T(8,128)(2,1)S(1)}, bf16[400,128]{1,0:T(8,128)(2,1)S(1)}, u32[]{:S(2)}, u32[]{:S(2)}) collective-permute-start(bf16[400,128]{1,0:T(8,128)(2,1)S(1)} %get-tuple-element.21.refs_0_), channel_id=1, source_target_pairs={{0,1},{1,0},{2,3},{3,2},{4,5},{5,4},{6,7},{7,6},{8,9},{9,8},{10,11... | collective-permute-start | bytes 307208 | tf_op jit(solution)/shard_map/ppermute | solution.py:439
  13.8 7.1 %collective-permute-start.4 = (bf16[400,128]{1,0:T(8,128)(2,1)S(1)}, bf16[400,128]{1,0:T(8,128)(2,1)S(1)}, u32[]{:S(2)}, u32[]{:S(2)}) collective-permute-start(bf16[400,128]{1,0:T(8,128)(2,1)S(1)} %get-tuple-element.21.refs_0_), channel_id=1, source_target_pairs={{0,2},{1,3},{2,0},{3,1},{4,6},{5,7},{6,4},{7,5},{8,10},{9,11},{10,... | collective-permute-start | bytes 307208 | tf_op jit(solution)/shard_map/ppermute | solution.py:439
  15.4 11.0 %collective-permute-start.5 = (bf16[400,128]{1,0:T(8,128)(2,1)S(1)}, bf16[400,128]{1,0:T(8,128)(2,1)S(1)}, u32[]{:S(2)}, u32[]{:S(2)}) collective-permute-start(bf16[400,128]{1,0:T(8,128)(2,1)S(1)} %get-tuple-element.21.refs_0_), channel_id=1, source_target_pairs={{0,16},{1,17},{2,18},{3,19},{4,20},{5,21},{6,22},{7,23},{8,24},{9,... | collective-permute-start | bytes 307208 | tf_op jit(solution)/shard_map/ppermute | solution.py:439
  16.9 1.2 %collective-permute-start.1 = (s32[1,1024]{1,0:T(1,128)S(1)}, s32[1,1024]{1,0:T(1,128)S(1)}, u32[]{:S(2)}, u32[]{:S(2)}) collective-permute-start(s32[1,1024]{1,0:T(1,128)S(1)} %copy-done.1), channel_id=1, source_target_pairs={{0,8},{8,0},{16,24},{24,16},{1,9},{9,1},{17,25},{25,17},{2,10},{10... | collective-permute-start | bytes 12296 | tf_op jit(solution)/shard_map/ppermute | solution.py:410
  18.0 9.4 %collective-permute-start.6 = (bf16[400,128]{1,0:T(8,128)(2,1)S(1)}, bf16[400,128]{1,0:T(8,128)(2,1)S(1)}, u32[]{:S(2)}, u32[]{:S(2)}) collective-permute-start(bf16[400,128]{1,0:T(8,128)(2,1)S(1)} %get-tuple-element.21.refs_0_), channel_id=1, source_target_pairs={{0,19},{1,18},{2,17},{3,16},{4,23},{5,22},{6,21},{7,20},{8,27},{9,... | collective-permute-start | bytes 307208 | tf_op jit(solution)/shard_map/ppermute | solution.py:439
  18.4 9.6 %collective-permute-start.7 = (bf16[400,128]{1,0:T(8,128)(2,1)S(1)}, bf16[400,128]{1,0:T(8,128)(2,1)S(1)}, u32[]{:S(2)}, u32[]{:S(2)}) collective-permute-start(bf16[400,128]{1,0:T(8,128)(2,1)S(1)} %get-tuple-element.21.refs_0_), channel_id=1, source_target_pairs={{0,3},{1,2},{2,1},{3,0},{4,7},{5,6},{6,5},{7,4},{8,11},{9,10},{10,... | collective-permute-start | bytes 307208 | tf_op jit(solution)/shard_map/ppermute | solution.py:439
  20.9 9.6 %collective-permute-start.8 = (bf16[400,128]{1,0:T(8,128)(2,1)S(1)}, bf16[400,128]{1,0:T(8,128)(2,1)S(1)}, u32[]{:S(2)}, u32[]{:S(2)}) collective-permute-start(bf16[400,128]{1,0:T(8,128)(2,1)S(1)} %get-tuple-element.21.refs_0_), channel_id=1, source_target_pairs={{0,17},{1,16},{2,19},{3,18},{4,21},{5,20},{6,23},{7,22},{8,25},{9,... | collective-permute-start | bytes 307208 | tf_op jit(solution)/shard_map/ppermute | solution.py:439
  22.4 1.2 %copy-start.2 = (bf16[1024,768]{1,0:T(8,128)(2,1)}, bf16[1024,768]{1,0:T(8,128)(2,1)S(1)}, u32[]{:S(2)}) copy-start(bf16[1024,768]{1,0:T(8,128)(2,1)S(1)} %collective-permute-done.2.store) | copy-start | bytes 4718596
  23.5 7.0 %collective-permute-start.9 = (bf16[400,128]{1,0:T(8,128)(2,1)S(1)}, bf16[400,128]{1,0:T(8,128)(2,1)S(1)}, u32[]{:S(2)}, u32[]{:S(2)}) collective-permute-start(bf16[400,128]{1,0:T(8,128)(2,1)S(1)} %get-tuple-element.21.refs_0_), channel_id=1, source_target_pairs={{0,18},{1,19},{2,16},{3,17},{4,22},{5,23},{6,20},{7,21},{8,26},{9,... | collective-permute-start | bytes 307208 | tf_op jit(solution)/shard_map/ppermute | solution.py:439
